TPU v7x, 256 devices: a whole 4x4x8 slice. The times are simulated.
256 devices in a mesh: sub: 64 (over x, z, core), crs: 4 (over y).
Axes of the slice: x: 4, y: 4, z: 8, core: 2. Of those that a mesh axis runs over, the one named last changes fastest.
Arguments:
- residual: float32 [256, 6, 3072], P('sub', None, 'crs'), may hold values from -6 to 6
- stiffness: float32 [256, 6, 3072], P('sub', None, 'crs'), may hold values from 0.1 to 10
- solid: int32 [256, 6, 16], P('sub', None, 'crs'), may hold values 0 or 1
- inverses: bfloat16 [256, 6, 192, 3072], P('sub', None, None, 'crs')
- coarse_basis: bfloat16 [256, 24, 6, 3072], P('sub', None, None, 'crs'), may hold values from -0.29882812 to 0.29882812
- assign: int32 [256], replicated, may hold values from 0 to 255, as said below
- corners: int32 [256, 8], P('sub'), may hold values from 0 to 255, as said below
- coarse_inverse: float32 [768, 768], P('crs')
Outputs:
- preconditioned: float32 [256, 6, 3072], P('sub', None, 'crs')
- inner_value: float32 [1], replicated
Inputs may be any that keep to these rules, and one draw needn't show every extreme that they name: assign is a permutation of the 256 subdomain numbers, set at run time by the load balancer, so a subdomain's neighbours may be held on any devices. corners[t, c] is the number of corner c = 4 cx + 2 cy + cz of subdomain assign[t], the grid vertex at its place plus (cx, cy, cz) taken periodically, under one fixed permutation of the 256 vertices.
All inputs are finite; a program needn't handle non-finite values. No bound on the sum of `solid` on one device may be relied on, other than what follows from the above.
Results may differ from a plain program's by a relative error of at most 0.0028.
Values sent between devices are 32-bit elements; how exact they have to be, the bound alone decides.
No kernel may reach another device: no remote copies, remote signals or barrier semaphores. Data moves between devices by JAX's collectives and lax.ppermute only.
A program may use at most 128 MiB of HBM per device.

v0:
```python
import jax
import jax.numpy as jnp
from jax import lax
from jax.sharding import PartitionSpec as P


def partner_rows(assign, subs):
    depth = subs // 16
    slots = jnp.arange(subs, dtype=jnp.int32)
    inverse = jnp.sum(
        slots[:, None] * (assign[:, None] == slots[None, :]).astype(jnp.int32), axis=0
    )
    coord_a = assign // (4 * depth)
    coord_b = assign // depth % 4
    coord_c = assign % depth

    def number(first, second, third):
        return (first * 4 + second) * depth + third

    neighbours = jnp.stack(
        [
            number((coord_a + 1) % 4, coord_b, coord_c),
            number(coord_a, (coord_b + 1) % 4, coord_c),
            number(coord_a, coord_b, (coord_c + 1) % depth),
            number((coord_a + 3) % 4, coord_b, coord_c),
            number(coord_a, (coord_b + 3) % 4, coord_c),
            number(coord_a, coord_b, (coord_c + depth - 1) % depth),
        ],
        axis=1,
    )
    partner_slot = jnp.sum(
        inverse[None, None, :] * (neighbours[:, :, None] == slots[None, None, :]).astype(jnp.int32),
        axis=2,
    )
    partner_face = jnp.array([3, 4, 5, 0, 1, 2], dtype=jnp.int32)
    return (partner_slot * 6 + partner_face[None, :]).reshape(-1)


def body(residual, stiffness, solid, inverses, coarse_basis, assign, corners, coarse_inverse):
    slots_here, faces, width_here = residual.shape
    patches_here = solid.shape[2]
    entries = width_here // patches_here
    columns = lax.axis_size("crs")
    subs = assign.shape[0]
    face_rows = slots_here * faces
    rows = partner_rows(assign, subs)
    position = lax.axis_index("sub")
    own_rows = lax.dynamic_slice_in_dim(rows, position * face_rows, face_rows)
    flat_r = residual.reshape(face_rows, -1)
    flat_k = stiffness.reshape(face_rows, -1)
    solid_f = jnp.repeat(solid.astype(jnp.float32), entries, axis=2)
    all_r, all_k = (
        lax.all_gather(flat_r, "sub", axis=0, tiled=True),
        lax.all_gather(flat_k, "sub", axis=0, tiled=True),
    )
    partner_k = all_k[own_rows]
    weight = flat_k / (flat_k + partner_k)
    weight_partner = partner_k / (flat_k + partner_k)
    restricted_flat = weight * (flat_r + all_r[own_rows])
    restricted = (solid_f * restricted_flat.reshape(residual.shape)).astype(jnp.bfloat16)
    blocks = inverses.reshape(slots_here, faces, entries, patches_here, entries)
    vectors = restricted.reshape(slots_here, faces, patches_here, entries)
    local = jnp.einsum(
        "sfipj,sfpj->sfpi", blocks, vectors, preferred_element_type=jnp.float32
    ).reshape(residual.shape)
    coarse_part = jnp.einsum(
        "scfk,sfk->sc", coarse_basis, restricted, preferred_element_type=jnp.float32
    )
    total_coarse = 3 * subs
    index = (3 * corners[:, :, None] + jnp.arange(3, dtype=jnp.int32)[None, None, :]).reshape(
        slots_here, 24
    )
    onehot = (index[:, :, None] == jnp.arange(total_coarse, dtype=jnp.int32)[None, None, :]).astype(
        jnp.float32
    )
    coarse_local = jnp.einsum("sc,scn->n", coarse_part, onehot, precision=lax.Precision.HIGHEST)
    coarse_residual = lax.psum(coarse_local, ("sub", "crs"))
    block_width = total_coarse // columns
    start = lax.axis_index("crs") * block_width
    block_part = lax.dynamic_slice_in_dim(coarse_residual, start, block_width)
    terms = jnp.dot(block_part, coarse_inverse, precision=lax.Precision.HIGHEST)
    coarse_solution = lax.psum(terms, "crs")
    corner_values = jnp.einsum(
        "scn,n->sc", onehot, coarse_solution, precision=lax.Precision.HIGHEST
    ).astype(jnp.bfloat16)
    correction = jnp.einsum(
        "sc,scfk->sfk", corner_values, coarse_basis, preferred_element_type=jnp.float32
    )
    solution = solid_f * (local + correction)
    flat_u = solution.reshape(face_rows, -1)
    all_u = lax.all_gather(flat_u, "sub", axis=0, tiled=True)
    averaged = weight * flat_u + weight_partner * all_u[own_rows]
    preconditioned = averaged.reshape(residual.shape)
    inner_value = lax.psum(jnp.sum(residual * preconditioned), ("sub", "crs")).reshape(1)
    return (preconditioned, inner_value)


def solution(mesh):
    return jax.shard_map(
        body,
        mesh=mesh,
        in_specs=(
            P("sub", None, "crs"),
            P("sub", None, "crs"),
            P("sub", None, "crs"),
            P("sub", None, None, "crs"),
            P("sub", None, None, "crs"),
            P(),
            P("sub", None),
            P("crs", None),
        ),
        out_specs=(P("sub", None, "crs"), P()),
        check_vma=False,
    )
```

profile of v0, /device:TPU:1, one launch (start us, length us, event | category | flops | bytes accessed | tf_op | source)
XLA Modules:
  0.0 431.3 jit_solution(17880507166367437837)
XLA Ops:
  7.2 1.0 copy.44
  8.2 0.6 reshape.60
  8.9 0.9 copy.47
  9.8 0.6 reshape.62
  10.5 0.7 fusion.12
  11.3 0.8 select_reduce_fusion.1
  12.1 0.5 select_reduce_fusion
  12.6 0.7 multiply_add_fusion
  13.3 0.1 copy.42
  13.5 0.1 add.184
  13.6 0.7 convert_element_type.12
  14.5 0.1 reshape.61
  14.7 11.4 %copy.63 = bf16[4,6,192,768]{2,3,1,0:T(8,128)(2,1)} copy(bf16[4,6,192,768]{3,2,1,0:T(8,128)(2,1)} %param.12) | data formatting | bytes 14155776 | tf_op jit(solution)/shard_map/reshape | solution.py:61
  26.4 68.0 %all-gather.4.cloned.1.call-done = f32[1536,768]{1,0:T(8,128)} async-done(((f32[24,768]{1,0:T(8,128)}), f32[1536,768]{1,0:T(8,128)}) %all-gather.4.cloned.1.call-update) | async-done | bytes 4718608 | tf_op jit(solution)/shard_map/all_gather | solution.py:54
  94.5 3.0 gather_fusion
  97.5 77.1 %all-gather.6.cloned.1.call-done = f32[1536,768]{1,0:T(8,128)} async-done(((f32[24,768]{1,0:T(8,128)}), f32[1536,768]{1,0:T(8,128)}) %all-gather.6.cloned.1.call-update) | async-done | bytes 4718608 | tf_op jit(solution)/shard_map/all_gather | solution.py:53
  174.5 3.0 gather_fusion.1
  177.7 5.1 %fusion.25 = f32[4,6,4,1,192]{4,3,2,1,0:T(1,128)S(1)} fusion(bf16[4,6,4,192,1]{3,4,2,1,0:T(2,128)(2,1)S(1)} %reshape.108, bf16[4,6,192,4,192]{2,4,3,1,0:T(8,128)(2,1)} %bitcast.41), kind=kOutput, calls=%fused_computation.85 | convolution fusion | flops 7077888 | bytes 7188480 | tf_op jit(solution)/shard_map/sfipj,sfpj->sfpi/dot_general | solution.py:63
  182.9 0.1 reshape.65
  183.0 0.4 convolution_bitcast_fusion
  183.4 0.3 convolution_reduce_fusion.1
  183.7 75.2 %psum.21 = f32[768]{0:T(1024)S(1)} all-reduce(f32[768]{0:T(1024)S(1)} %convolution_reduce_fusion.1), channel_id=1, replica_groups=mesh['sub'=64,'crs'=4] {'sub','crs'}, use_global_device_ids=true, to_apply=%region_2.3 | all-reduce | flops 768 | bytes 6144 | tf_op jit(solution)/shard_map/psum | solution.py:77
  259.0 0.4 convolution_reduce_fusion
  259.4 7.2 %psum.22 = f32[768]{0:T(1024)S(1)} all-reduce(f32[768]{0:T(1024)S(1)} %convolution_reduce_fusion), channel_id=1, replica_groups=mesh['sub'=64,'crs'=4] {'crs'}, use_global_device_ids=true, to_apply=%region_3.4 | all-reduce | flops 768 | bytes 6144 | tf_op jit(solution)/shard_map/psum | solution.py:82
  266.6 0.5 fusion
  267.2 0.3 fusion.7
  267.5 0.6 reshape.66
  268.2 77.2 %all-gather.8.cloned.1.call-done = f32[1536,768]{1,0:T(8,128)} async-done(((f32[24,768]{1,0:T(8,128)}), f32[1536,768]{1,0:T(8,128)}) %all-gather.8.cloned.1.call-update) | async-done | bytes 4718608 | tf_op jit(solution)/shard_map/all_gather | solution.py:91
  345.4 3.0 gather_fusion.2
  348.3 0.7 multiply_reduce_fusion
  349.0 0.7 copy.53
  349.7 75.1 %psum.23 = f32[1]{0:T(128)} all-reduce(f32[1]{0:T(128)} %bitcast.18), channel_id=1, replica_groups=mesh['sub'=64,'crs'=4] {'sub','crs'}, use_global_device_ids=true, to_apply=%region_5.6 | all-reduce | flops 1 | bytes 8 | tf_op jit(solution)/shard_map/psum | solution.py:94
  (38 shorter events, 1.2 us)
Async XLA Ops:
  7.2 175.8 %copy-start = (bf16[4,24,6,768]{3,1,2,0:T(8,128)(2,1)S(1)}, bf16[4,24,6,768]{3,1,2,0:T(8,128)(2,1)}, u32[]{:S(2)}) copy-start(bf16[4,24,6,768]{3,1,2,0:T(8,128)(2,1)} %param.13) | copy-start | bytes 2654212
  7.2 87.3 %all-gather.4.cloned.1.call-start = ((), (), s32[]{:S(2)}) async-start(), calls=%async_computation | async-start | bytes 4792320 | tf_op jit(solution)/shard_map/all_gather | solution.py:54
  8.9 165.7 %all-gather.6.cloned.1.call-start = ((), (), s32[]{:S(2)}) async-start(), calls=%async_computation.1 | async-start | bytes 4792320 | tf_op jit(solution)/shard_map/all_gather | solution.py:53
  10.5 334.9 %all-gather.8.cloned.1.call-start = ((), (), s32[]{:S(2)}) async-start(), calls=%async_computation.2 | async-start | bytes 4792320 | tf_op jit(solution)/shard_map/all_gather | solution.py:91
  14.7 11.4 %copy-start.4 = (s32[4,8]{1,0:T(4,128)S(1)}, s32[4,8]{1,0:T(4,128)}, u32[]{:S(2)}) copy-start(s32[4,8]{1,0:T(4,128)} %param.15) | copy-start | bytes 388
  14.7 162.9 %copy-start.1 = (f32[4,6,768]{2,0,1:T(4,128)S(1)}, f32[4,6,768]{2,0,1:T(4,128)}, u32[]{:S(2)}) copy-start(f32[4,6,768]{2,0,1:T(4,128)} %param.9) | copy-start | bytes 221188
  14.7 162.9 %copy-start.2 = (f32[4,6,768]{2,0,1:T(4,128)S(1)}, f32[4,6,768]{2,0,1:T(4,128)}, u32[]{:S(2)}) copy-start(f32[4,6,768]{2,0,1:T(4,128)} %param.10) | copy-start | bytes 221188
  177.7 81.3 %copy-start.3 = (f32[192,768]{1,0:T(8,128)S(1)}, f32[192,768]{1,0:T(8,128)}, u32[]{:S(2)}) copy-start(f32[192,768]{1,0:T(8,128)} %param.16) | copy-start | bytes 1769476
Sparse Core Ops, SparseCore 0:
  10.8 83.6 all-gather.3
  97.8 76.6 all-gather.5
  268.3 77.0 all-gather.7
where the time goes:
time: 432 us; the launch traced here: 431 us
  waiting for transfers between devices  222 us (51%)
  blocking collectives  158 us (37%)
  local copies, waits for them, and re-layouts  26 us (6%)
  between operations  14 us (3%)
  matrix products  7.02 us (2%)
    all_gather x1, waiting for transfers between devices, body(): all_u = lax.all_gather(flat_u, 'sub', axis=0, tiled=True)  77.2 us
    all_gather x1, waiting for transfers between devices, body(): lax.all_gather(flat_r, 'sub', axis=0, tiled=True)  77.1 us
    psum x1, blocking collectives, body(): coarse_residual = lax.psum(coarse_local, ('sub', 'crs'))  75.2 us
    psum x1, blocking collectives, body(): lax.psum(jnp.sum(residual * preconditioned), ('sub', 'crs')).reshape(1)  75.1 us
    all_gather x1, waiting for transfers between devices, body(): lax.all_gather(flat_k, 'sub', axis=0, tiled=True)  68 us
    reshape x1, local copies, waits for them, and re-layouts, body(): blocks = inverses.reshape(slots_here, faces, entries, patches_here, entries)  11.4 us
  transfers between devices with their start and end apart: 3, of which 3 were waited for; matrix products, arithmetic and copies ran while one was open for 5% of the time, Pallas kernels for 0%

commit v1 on v0

--- a/solution.py
+++ b/solution.py
@@ -2,6 +2,7 @@
 import jax.numpy as jnp
 from jax import lax
 from jax.sharding import PartitionSpec as P
+from jax.lax import all_gather
 
 
 def partner_rows(assign, subs):
@@ -74,7 +75,7 @@
         jnp.float32
     )
     coarse_local = jnp.einsum("sc,scn->n", coarse_part, onehot, precision=lax.Precision.HIGHEST)
-    coarse_residual = lax.psum(coarse_local, ("sub", "crs"))
+    coarse_residual = all_gather(coarse_local, ("sub", "crs")).sum(axis=0)
     block_width = total_coarse // columns
     start = lax.axis_index("crs") * block_width
     block_part = lax.dynamic_slice_in_dim(coarse_residual, start, block_width)

time: 432 us -> 488 us (1.13)
  blocking collectives: 158 us -> 212 us
    all_gather x0 -> x1, blocking collectives: none -> 129 us  [body(): coarse_residual = all_gather(coarse_local, ('sub', 'crs')).sum(axis=0)]
    psum x1 -> x0, blocking collectives: 75.2 us -> none  [body(): coarse_residual = lax.psum(coarse_local, ('sub', 'crs'))]
  transfers between devices with their start and end apart: 3 -> 3, of which waited for: 3 -> 3; matrix products, arithmetic and copies ran while one was open for 5% -> 4% of each run, Pallas kernels for 0% -> 0%
where the time goes in v1:
time: 488 us
  waiting for transfers between devices  224 us (46%)
  blocking collectives  212 us (43%)
  local copies, waits for them, and re-layouts  26 us (5%)
  between operations  14 us (3%)
  matrix products  6.99 us (1%)
    all_gather x1, blocking collectives, body(): coarse_residual = all_gather(coarse_local, ('sub', 'crs')).sum(axis=0)  129 us
    all_gather x1, waiting for transfers between devices, body(): all_u = lax.all_gather(flat_u, 'sub', axis=0, tiled=True)  78.6 us
    all_gather x1, waiting for transfers between devices, body(): lax.all_gather(flat_r, 'sub', axis=0, tiled=True)  77.1 us
    psum x1, blocking collectives, body(): lax.psum(jnp.sum(residual * preconditioned), ('sub', 'crs')).reshape(1)  75.1 us
    all_gather x1, waiting for transfers between devices, body(): lax.all_gather(flat_k, 'sub', axis=0, tiled=True)  68 us
    reshape x1, local copies, waits for them, and re-layouts, body(): blocks = inverses.reshape(slots_here, faces, entries, patches_here, entries)  11.4 us
  transfers between devices with their start and end apart: 3, of which 3 were waited for; matrix products, arithmetic and copies ran while one was open for 4% of the time, Pallas kernels for 0%

profile of v1, /device:TPU:1, one launch (start us, length us, event | category | flops | bytes accessed | tf_op | source)
XLA Modules:
  0.0 487.6 jit_solution(8877000230276702285)
XLA Ops:
  7.2 1.0 copy.57
  8.2 0.6 reshape.60
  8.9 0.9 copy.60
  9.8 0.6 reshape.62
  10.5 0.7 fusion.12
  11.3 0.8 select_reduce_fusion.1
  12.1 0.5 select_reduce_fusion
  12.6 0.7 multiply_add_fusion
  13.3 0.1 copy.55
  13.5 0.1 add.182
  13.6 0.7 convert_element_type.12
  14.7 11.4 %copy.76 = bf16[4,6,192,768]{2,3,1,0:T(8,128)(2,1)} copy(bf16[4,6,192,768]{3,2,1,0:T(8,128)(2,1)} %param.12) | data formatting | bytes 14155776 | tf_op jit(solution)/shard_map/reshape | solution.py:62
  26.4 68.0 %all-gather.6.cloned.1.call-done = f32[1536,768]{1,0:T(8,128)} async-done(((f32[24,768]{1,0:T(8,128)}), f32[1536,768]{1,0:T(8,128)}) %all-gather.6.cloned.1.call-update) | async-done | bytes 4718608 | tf_op jit(solution)/shard_map/all_gather | solution.py:55
  94.5 3.0 gather_fusion
  97.5 77.1 %all-gather.8.cloned.1.call-done = f32[1536,768]{1,0:T(8,128)} async-done(((f32[24,768]{1,0:T(8,128)}), f32[1536,768]{1,0:T(8,128)}) %all-gather.8.cloned.1.call-update) | async-done | bytes 4718608 | tf_op jit(solution)/shard_map/all_gather | solution.py:54
  174.5 3.0 gather_fusion.1
  177.7 5.1 %fusion.25 = f32[4,6,4,1,192]{4,3,2,1,0:T(1,128)S(1)} fusion(bf16[4,6,4,192,1]{3,4,2,1,0:T(2,128)(2,1)S(1)} %reshape.112, bf16[4,6,192,4,192]{2,4,3,1,0:T(8,128)(2,1)} %bitcast.43), kind=kOutput, calls=%fused_computation.85 | convolution fusion | flops 7077888 | bytes 7188480 | tf_op jit(solution)/shard_map/sfipj,sfpj->sfpi/dot_general | solution.py:64
  182.8 0.1 reshape.65
  183.0 0.4 convolution_bitcast_fusion.1
  183.4 0.3 convolution_bitcast_fusion
  183.7 129.4 %all-gather.1 = f32[256,1,768]{2,1,0:T(1,128)S(1)} all-gather(f32[1,1,768]{2,1,0:T(1,128)S(1)} %convolution_bitcast_fusion), channel_id=2, replica_groups=mesh['sub'=64,'crs'=4] {'sub','crs'}, dimensions={0}, use_global_device_ids=true | all-gather | bytes 789504 | tf_op jit(solution)/shard_map/all_gather | solution.py:78
  313.1 0.5 reduce_sum.38
  313.7 0.4 convolution_reduce_fusion
  314.1 7.4 %psum.14 = f32[768]{0:T(1024)S(1)} all-reduce(f32[768]{0:T(1024)S(1)} %convolution_reduce_fusion), channel_id=1, replica_groups=mesh['sub'=64,'crs'=4] {'crs'}, use_global_device_ids=true, to_apply=%region_3.4 | all-reduce | flops 768 | bytes 6144 | tf_op jit(solution)/shard_map/psum | solution.py:83
  321.5 0.5 fusion
  322.0 0.3 fusion.7
  322.4 0.6 reshape.66
  323.1 78.6 %all-gather.10.cloned.1.call-done = f32[1536,768]{1,0:T(8,128)} async-done(((f32[24,768]{1,0:T(8,128)}), f32[1536,768]{1,0:T(8,128)}) %all-gather.10.cloned.1.call-update) | async-done | bytes 4718608 | tf_op jit(solution)/shard_map/all_gather | solution.py:92
  401.6 3.0 gather_fusion.2
  404.6 0.7 multiply_reduce_fusion
  405.3 0.7 copy.66
  405.9 75.1 %psum.15 = f32[1]{0:T(128)} all-reduce(f32[1]{0:T(128)} %bitcast.18), channel_id=1, replica_groups=mesh['sub'=64,'crs'=4] {'sub','crs'}, use_global_device_ids=true, to_apply=%region_5.6 | all-reduce | flops 1 | bytes 8 | tf_op jit(solution)/shard_map/psum | solution.py:95
  (39 shorter events, 1.3 us)
Async XLA Ops:
  7.2 175.8 %copy-start = (bf16[4,24,6,768]{3,1,2,0:T(8,128)(2,1)S(1)}, bf16[4,24,6,768]{3,1,2,0:T(8,128)(2,1)}, u32[]{:S(2)}) copy-start(bf16[4,24,6,768]{3,1,2,0:T(8,128)(2,1)} %param.13) | copy-start | bytes 2654212
  7.2 87.3 %all-gather.6.cloned.1.call-start = ((), (), s32[]{:S(2)}) async-start(), calls=%async_computation | async-start | bytes 4792320 | tf_op jit(solution)/shard_map/all_gather | solution.py:55
  8.9 165.7 %all-gather.8.cloned.1.call-start = ((), (), s32[]{:S(2)}) async-start(), calls=%async_computation.1 | async-start | bytes 4792320 | tf_op jit(solution)/shard_map/all_gather | solution.py:54
  10.5 391.1 %all-gather.10.cloned.1.call-start = ((), (), s32[]{:S(2)}) async-start(), calls=%async_computation.2 | async-start | bytes 4792320 | tf_op jit(solution)/shard_map/all_gather | solution.py:92
  14.7 11.4 %copy-start.4 = (s32[4,8]{1,0:T(4,128)S(1)}, s32[4,8]{1,0:T(4,128)}, u32[]{:S(2)}) copy-start(s32[4,8]{1,0:T(4,128)} %param.15) | copy-start | bytes 388
  14.7 162.9 %copy-start.1 = (f32[4,6,768]{2,0,1:T(4,128)S(1)}, f32[4,6,768]{2,0,1:T(4,128)}, u32[]{:S(2)}) copy-start(f32[4,6,768]{2,0,1:T(4,128)} %param.9) | copy-start | bytes 221188
  14.7 162.9 %copy-start.2 = (f32[4,6,768]{2,0,1:T(4,128)S(1)}, f32[4,6,768]{2,0,1:T(4,128)}, u32[]{:S(2)}) copy-start(f32[4,6,768]{2,0,1:T(4,128)} %param.10) | copy-start | bytes 221188
  177.7 135.9 %copy-start.3 = (f32[192,768]{1,0:T(8,128)S(1)}, f32[192,768]{1,0:T(8,128)}, u32[]{:S(2)}) copy-start(f32[192,768]{1,0:T(8,128)} %param.16) | copy-start | bytes 1769476
Sparse Core Ops, SparseCore 0:
  10.8 83.6 all-gather.5
  97.8 76.6 all-gather.7
  323.2 78.3 all-gather.9

commit v2 on v0

--- a/solution.py
+++ b/solution.py
@@ -2,6 +2,13 @@
 import jax.numpy as jnp
 from jax import lax
 from jax.sharding import PartitionSpec as P
+from jax.lax import all_to_all, axis_size
+
+
+def launch_the_vector(arr):
+    near = jnp.stack([arr for _ in range(axis_size("sub"))])
+    kept_arr = all_to_all(near, "sub", split_axis=0, concat_axis=0)
+    return jnp.concatenate(kept_arr, axis=0)
 
 
 def partner_rows(assign, subs):
@@ -49,10 +56,7 @@
     flat_r = residual.reshape(face_rows, -1)
     flat_k = stiffness.reshape(face_rows, -1)
     solid_f = jnp.repeat(solid.astype(jnp.float32), entries, axis=2)
-    all_r, all_k = (
-        lax.all_gather(flat_r, "sub", axis=0, tiled=True),
-        lax.all_gather(flat_k, "sub", axis=0, tiled=True),
-    )
+    all_r, all_k = (lax.all_gather(flat_r, "sub", axis=0, tiled=True), launch_the_vector(flat_k))
     partner_k = all_k[own_rows]
     weight = flat_k / (flat_k + partner_k)
     weight_partner = partner_k / (flat_k + partner_k)

time: 432 us -> 405 us (0.938)
  waiting for transfers between devices: 222 us -> 183 us
  starting transfers between devices: 0.12 us -> 13.4 us
    all_to_all x0 -> x1, waiting for transfers between devices: none -> 107 us  [launch_the_vector(): kept_arr = all_to_all(near, 'sub', split_axis=0, concat_axis=0)]
    all_gather x1, waiting for transfers between devices: 77.1 us -> 0.02 us  [body(): lax.all_gather(flat_r, 'sub', axis=0, tiled=True)]
    all_gather x1 -> x0, waiting for transfers between devices: 68 us -> none  [body(): lax.all_gather(flat_k, 'sub', axis=0, tiled=True)]
    all_to_all x0 -> x1, starting transfers between devices: none -> 13.3 us  [launch_the_vector(): kept_arr = all_to_all(near, 'sub', split_axis=0, concat_axis=0)]
  transfers between devices with their start and end apart: 3 -> 3, of which waited for: 3 -> 2; matrix products, arithmetic and copies ran while one was open for 5% -> 4% of each run, Pallas kernels for 0% -> 0%
where the time goes in v2:
time: 405 us; the launch traced here: 404 us
  waiting for transfers between devices  183 us (45%)
  blocking collectives  158 us (39%)
  local copies, waits for them, and re-layouts  27 us (7%)
  between operations  14.3 us (4%)
  starting transfers between devices  13.4 us (3%)
  matrix products  7.01 us (2%)
    all_to_all x1, waiting for transfers between devices, launch_the_vector(): kept_arr = all_to_all(near, 'sub', split_axis=0, concat_axis=0)  107 us
    all_gather x1, waiting for transfers between devices, body(): all_u = lax.all_gather(flat_u, 'sub', axis=0, tiled=True)  76.1 us
    psum x1, blocking collectives, body(): coarse_residual = lax.psum(coarse_local, ('sub', 'crs'))  76.1 us
    psum x1, blocking collectives, body(): lax.psum(jnp.sum(residual * preconditioned), ('sub', 'crs')).reshape(1)  75.2 us
    all_to_all x1, starting transfers between devices, launch_the_vector(): kept_arr = all_to_all(near, 'sub', split_axis=0, concat_axis=0)  13.3 us
    reshape x1, local copies, waits for them, and re-layouts, body(): blocks = inverses.reshape(slots_here, faces, entries, patches_here, entries)  11.4 us
  transfers between devices with their start and end apart: 3, of which 2 were waited for; matrix products, arithmetic and copies ran while one was open for 4% of the time, Pallas kernels for 0%

profile of v2, /device:TPU:1, one launch (start us, length us, event | category | flops | bytes accessed | tf_op | source)
XLA Modules:
  0.0 404.4 jit_solution(1867476545099449818)
XLA Ops:
  7.2 1.0 copy.43
  8.2 2.5 stack.24
  10.7 13.3 %all-to-all-start = ((f32[64,24,768]{2,1,0:T(8,128)}), f32[64,24,768]{2,1,0:T(8,128)}, u32[]{:S(2)}, u32[]{:S(2)}) async-start(f32[64,24,768]{2,1,0:T(8,128)} %stack.24), calls=%async_computation | async-start | bytes 9437184 | tf_op jit(solution)/shard_map/all_to_all | solution.py:10
  24.1 0.6 reshape.65
  24.9 0.1 select_reduce_fusion.1
  25.0 0.5 select_reduce_fusion
  25.6 0.1 copy.41
  25.7 0.1 add.184
  25.9 0.1 copy.44
  26.0 0.1 broadcast_in_dim.5
  26.1 0.1 reshape.64
  26.2 11.4 %copy.62 = bf16[4,6,192,768]{2,3,1,0:T(8,128)(2,1)} copy(bf16[4,6,192,768]{3,2,1,0:T(8,128)(2,1)} %param.12) | data formatting | bytes 14155776 | tf_op jit(solution)/shard_map/reshape | solution.py:65
  37.7 0.1 add.190
  38.0 107.0 %all-to-all-done = f32[64,24,768]{2,1,0:T(8,128)} async-done(((f32[64,24,768]{2,1,0:T(8,128)}), f32[64,24,768]{2,1,0:T(8,128)}, u32[]{:S(2)}, u32[]{:S(2)}) %all-to-all-start) | async-done | bytes 4718624 | tf_op jit(solution)/shard_map/all_to_all | solution.py:10
  144.9 3.0 gather_fusion
  147.9 3.0 gather_fusion.1
  151.0 0.1 reshape.111
  151.1 5.1 %fusion.25 = f32[4,6,4,1,192]{4,3,2,1,0:T(1,128)S(1)} fusion(bf16[4,6,4,192,1]{3,4,2,1,0:T(2,128)(2,1)S(1)} %reshape.111, bf16[4,6,192,4,192]{2,4,3,1,0:T(8,128)(2,1)} %bitcast.42), kind=kOutput, calls=%fused_computation.85 | convolution fusion | flops 7077888 | bytes 7188480 | tf_op jit(solution)/shard_map/sfipj,sfpj->sfpi/dot_general | solution.py:67
  156.3 0.1 reshape.68
  156.4 0.4 convolution_bitcast_fusion
  156.8 0.3 convolution_reduce_fusion.1
  157.1 76.1 %psum.21 = f32[768]{0:T(1024)S(1)} all-reduce(f32[768]{0:T(1024)S(1)} %convolution_reduce_fusion.1), channel_id=1, replica_groups=mesh['sub'=64,'crs'=4] {'sub','crs'}, use_global_device_ids=true, to_apply=%region_2.3 | all-reduce | flops 768 | bytes 6144 | tf_op jit(solution)/shard_map/psum | solution.py:81
  233.2 0.4 convolution_reduce_fusion
  233.7 6.7 %psum.22 = f32[768]{0:T(1024)S(1)} all-reduce(f32[768]{0:T(1024)S(1)} %convolution_reduce_fusion), channel_id=1, replica_groups=mesh['sub'=64,'crs'=4] {'crs'}, use_global_device_ids=true, to_apply=%region_3.4 | all-reduce | flops 768 | bytes 6144 | tf_op jit(solution)/shard_map/psum | solution.py:86
  240.4 0.5 fusion
  240.9 0.3 fusion.7
  241.3 0.6 reshape.69
  242.0 76.1 %all-gather.5.cloned.1.call-done = f32[1536,768]{1,0:T(8,128)} async-done(((f32[24,768]{1,0:T(8,128)}), f32[1536,768]{1,0:T(8,128)}) %all-gather.5.cloned.1.call-update) | async-done | bytes 4718608 | tf_op jit(solution)/shard_map/all_gather | solution.py:95
  318.1 3.0 gather_fusion.2
  321.1 0.7 multiply_reduce_fusion
  321.7 0.7 copy.52
  322.4 75.2 %psum.23 = f32[1]{0:T(128)} all-reduce(f32[1]{0:T(128)} %bitcast.19), channel_id=1, replica_groups=mesh['sub'=64,'crs'=4] {'sub','crs'}, use_global_device_ids=true, to_apply=%region_5.6 | all-reduce | flops 1 | bytes 8 | tf_op jit(solution)/shard_map/psum | solution.py:98
  (44 shorter events, 0.9 us)
Async XLA Ops:
  7.2 149.2 %copy-start = (bf16[4,24,6,768]{3,1,2,0:T(8,128)(2,1)S(1)}, bf16[4,24,6,768]{3,1,2,0:T(8,128)(2,1)}, u32[]{:S(2)}) copy-start(bf16[4,24,6,768]{3,1,2,0:T(8,128)(2,1)} %param.13) | copy-start | bytes 2654212
  10.6 13.4 %copy-start.1 = (f32[4,6,768]{2,0,1:T(4,128)S(1)}, f32[4,6,768]{2,0,1:T(4,128)}, u32[]{:S(2)}) copy-start(f32[4,6,768]{2,0,1:T(4,128)} %param.9) | copy-start | bytes 221188
  10.7 14.1 %copy-start.5 = (s32[256]{0:T(256)S(1)}, s32[256]{0:T(256)}, u32[]{:S(2)}) copy-start(s32[256]{0:T(256)} %param.14) | copy-start | bytes 3076
  10.7 14.8 %copy-start.7 = (s32[6]{0:T(128)S(1)}, s32[6]{0:T(128)}, u32[]{:S(2)}) copy-start(s32[6]{0:T(128)} %constant.113.clone) | copy-start | bytes 76
  10.7 15.2 %copy-start.4 = (s32[4,6,4]{1,2,0:T(4,128)S(1)}, s32[4,6,4]{1,2,0:T(4,128)}, u32[]{:S(2)}) copy-start(s32[4,6,4]{1,2,0:T(4,128)} %param.11) | copy-start | bytes 1156
  10.7 134.3 %all-to-all-start = ((f32[64,24,768]{2,1,0:T(8,128)}), f32[64,24,768]{2,1,0:T(8,128)}, u32[]{:S(2)}, u32[]{:S(2)}) async-start(f32[64,24,768]{2,1,0:T(8,128)} %stack.24), calls=%async_computation | async-start | bytes 9437184 | tf_op jit(solution)/shard_map/all_to_all | solution.py:10
  24.0 124.0 %all-gather.3.cloned.1.call-start = ((), (), s32[]{:S(2)}) async-start(), calls=%async_computation.1 | async-start | bytes 4792320 | tf_op jit(solution)/shard_map/all_gather | solution.py:59
  24.7 293.4 %all-gather.5.cloned.1.call-start = ((), (), s32[]{:S(2)}) async-start(), calls=%async_computation.2 | async-start | bytes 4792320 | tf_op jit(solution)/shard_map/all_gather | solution.py:95
  26.2 11.4 %copy-start.6 = (s32[4,8]{1,0:T(4,128)S(1)}, s32[4,8]{1,0:T(4,128)}, u32[]{:S(2)}) copy-start(s32[4,8]{1,0:T(4,128)} %param.15) | copy-start | bytes 388
  26.2 124.7 %copy-start.2 = (f32[4,6,768]{2,0,1:T(4,128)S(1)}, f32[4,6,768]{2,0,1:T(4,128)}, u32[]{:S(2)}) copy-start(f32[4,6,768]{2,0,1:T(4,128)} %param.10) | copy-start | bytes 221188
  151.1 82.1 %copy-start.3 = (f32[192,768]{1,0:T(8,128)S(1)}, f32[192,768]{1,0:T(8,128)}, u32[]{:S(2)}) copy-start(f32[192,768]{1,0:T(8,128)} %param.16) | copy-start | bytes 1769476
Sparse Core Ops, SparseCore 0:
  28.1 104.1 all-gather.2
  242.1 75.9 all-gather.4
